TPU v7x, 32 devices: a whole 2x2x4 slice. The times are simulated.
32 devices in a mesh: members: 2 (over y), tiles: 4 (over z), chan: 2 (over x), dirs: 2 (over core).
Axes of the slice: x: 2, y: 2, z: 4, core: 2. Of those that a mesh axis runs over, the one named last changes fastest.
Arguments:
- field: float32 [64, 128, 256], P(('members', 'tiles'), 'chan'), parts along dimension 0, may hold values from -6 to 6
- tangents: float32 [4, 64, 128, 256], P('dirs', ('members', 'tiles'), 'chan'), parts along dimension 1, may hold values from -6 to 6
- weight_one: float32 [9, 128, 128], replicated, may hold values from -0.1875 to 0.1875
- bias_one: float32 [128], replicated, may hold values from -3 to 3
- weight_two: float32 [9, 128, 128], replicated, may hold values from -0.1875 to 0.1875
- bias_two: float32 [128], replicated, may hold values from -3 to 3
- adjacency: int32 [32, 4], replicated, may hold values from 0 to 31
- side_code: int32 [32, 4], replicated, may hold values from 0 to 3
- mirror_flag: int32 [32, 4], replicated, may hold values from 0 to 1
- placement: int32 [32], replicated, may hold values from 0 to 31, each once
Outputs:
- output: float32 [64, 128, 256], P(('members', 'tiles'), 'chan'), parts along dimension 0
- output_tangents: float32 [4, 64, 128, 256], P('dirs', ('members', 'tiles'), 'chan'), parts along dimension 1
There are 2 independent parts, one for each index of `members`. A program takes and returns all parts, laid end to end along the dimension named above; an argument that names none is the same for every part. Nothing has to cross between parts.
Inputs may be any that keep to these rules, and one draw needn't show every extreme that they name: `adjacency`: tile ids; a tile may border itself or the same tile on several sides. `placement`: every tile id once.
All inputs are finite; a program needn't handle non-finite values.
Results may differ from a plain program's by a relative error of at most 0.00011.
Values sent between devices are 32-bit elements; how exact they have to be, the bound alone decides.
No kernel may reach another device: no remote copies, remote signals or barrier semaphores. Data moves between devices by JAX's collectives and lax.ppermute only.
A program may use at most 128 MiB of HBM per device.

v0:
```python
import jax
import jax.numpy as jnp
import numpy as np
from jax import lax
from jax.sharding import PartitionSpec as P

S = 16


def static_tables():
    width = S + 2
    length = width * width + 2
    where_at = np.arange(length)
    row_at = where_at // width
    col_at = where_at % width
    inside = where_at < width * width
    mid_row = (row_at >= 1) & (row_at <= S)
    mid_col = (col_at >= 1) & (col_at <= S)
    side_at = np.full(length, 4)
    along = np.zeros(length, dtype=np.int64)
    side_at = np.where(inside & (row_at == 0) & mid_col, 0, side_at)
    side_at = np.where(inside & (row_at == S + 1) & mid_col, 1, side_at)
    side_at = np.where(inside & (col_at == 0) & mid_row, 2, side_at)
    side_at = np.where(inside & (col_at == S + 1) & mid_row, 3, side_at)
    side_at = np.where(inside & mid_row & mid_col, -1, side_at)
    along = np.where((side_at == 0) | (side_at == 1), col_at - 1, along)
    along = np.where((side_at == 2) | (side_at == 3), row_at - 1, along)
    along = np.where(side_at == -1, (row_at - 1) * S + (col_at - 1), along)
    return (side_at.astype(np.int32), along.astype(np.int32))


def pad_index(flips):
    side_np, along_np = static_tables()
    side_at = jnp.asarray(side_np)
    along = jnp.asarray(along_np)
    side_safe = jnp.clip(side_at, 0, 3)
    flip_at = jnp.take(flips, side_safe, axis=1)
    rim_index = (
        S * S
        + side_safe[None, :] * S
        + jnp.where(flip_at == 1, S - 1 - along[None, :], along[None, :])
    )
    zero_index = S * S + 4 * S
    index = jnp.where(
        side_at[None, :] == -1,
        along[None, :],
        jnp.where(side_at[None, :] == 4, zero_index, rim_index),
    )
    return index.astype(jnp.int32)


def convolve(padded, weight):
    tap_count = weight.shape[0]
    out_count = weight.shape[1]
    width = S + 2
    span = S * width
    flat_weight = weight.reshape(tap_count * out_count, weight.shape[2])
    planes = jnp.einsum("kc,btcl->btkl", flat_weight, padded, precision=lax.Precision.HIGHEST)
    planes = planes.reshape(padded.shape[0], padded.shape[1], tap_count, out_count, padded.shape[3])
    summed = None
    for row_off in range(3):
        for col_off in range(3):
            offset = row_off * width + col_off
            term = planes[:, :, row_off * 3 + col_off, :, offset : offset + span]
            summed = term if summed is None else summed + term
    keep_np = (np.arange(S)[:, None] * width + np.arange(S)[None, :]).reshape(-1).astype(np.int32)
    return jnp.take(summed, jnp.asarray(keep_np), axis=-1)


def pad_fields(fields, near_slot, codes, index):
    stream_count = fields.shape[0]
    tile_count = fields.shape[1]
    chan_count = fields.shape[2]
    grid_view = fields.reshape(stream_count, tile_count, chan_count, S, S)
    edges = jnp.stack(
        [
            grid_view[..., 0, :],
            grid_view[..., S - 1, :],
            grid_view[..., :, 0],
            grid_view[..., :, S - 1],
        ],
        axis=2,
    )
    everyone = lax.all_gather(
        edges.reshape(stream_count, tile_count, 4 * chan_count * S), "tiles", axis=1, tiled=True
    )
    flat_edges = everyone.reshape(stream_count, everyone.shape[1] * 4, chan_count * S)
    lookup = (near_slot * 4 + codes).reshape(-1)
    rims = jnp.take(flat_edges, lookup, axis=1).reshape(stream_count, tile_count, 4, chan_count, S)
    rims = jnp.transpose(rims, (0, 1, 3, 2, 4)).reshape(stream_count, tile_count, chan_count, 4 * S)
    zeros_col = jnp.zeros((stream_count, tile_count, chan_count, 1), jnp.float32)
    source = jnp.concatenate([fields, rims, zeros_col], axis=-1)
    return jnp.take_along_axis(source, index[None, :, None, :], axis=-1)


def layer_sums(padded, weight):
    chan_group = padded.shape[2]
    chan_start = lax.axis_index("chan") * chan_group
    weight_rows = lax.dynamic_slice_in_dim(weight, chan_start, chan_group, 1)
    gathered = lax.all_gather(padded, "chan", axis=2, tiled=True)
    return convolve(gathered, weight_rows)


def local(
    field,
    tangents,
    weight_one,
    bias_one,
    weight_two,
    bias_two,
    adjacency,
    side_code,
    mirror_flag,
    placement,
):
    tile_count = field.shape[0]
    chan_group = field.shape[1]
    total_tiles = placement.shape[0]
    ident = jnp.arange(total_tiles, dtype=jnp.int32)
    slot_of = jnp.sum(jnp.where(placement[None, :] == ident[:, None], ident[None, :], 0), axis=1)
    mine = lax.dynamic_slice_in_dim(placement, lax.axis_index("tiles") * tile_count, tile_count)
    near_slot = jnp.take(slot_of, jnp.take(adjacency, mine, axis=0).reshape(-1), axis=0).reshape(
        tile_count, 4
    )
    codes = jnp.take(side_code, mine, axis=0)
    flips = jnp.take(mirror_flag, mine, axis=0)
    index = pad_index(flips)
    chan_start = lax.axis_index("chan") * chan_group
    streams = jnp.concatenate([field[None], tangents], axis=0)
    weights = (weight_one, weight_two)
    biases = (
        lax.dynamic_slice_in_dim(bias_one, chan_start, chan_group),
        lax.dynamic_slice_in_dim(bias_two, chan_start, chan_group),
    )
    result = None
    for layer in range(2):
        summed = layer_sums(pad_fields(streams, near_slot, codes, index), weights[layer])
        pre = summed[0] + biases[layer][:, None]
        if layer == 0:
            sigma = jax.nn.sigmoid(pre)
            slope = sigma * (1.0 + pre * (1.0 - sigma))
            streams = jnp.concatenate([(pre * sigma)[None], summed[1:] * slope[None]], axis=0)
        else:
            result = (pre, summed[1:])
    return result


def solution(mesh):
    placed = (
        P(("members", "tiles"), "chan", None),
        P("dirs", ("members", "tiles"), "chan", None),
        P(),
        P(),
        P(),
        P(),
        P(),
        P(),
        P(),
        P(),
    )
    return jax.shard_map(
        local,
        mesh=mesh,
        in_specs=placed,
        out_specs=(
            P(("members", "tiles"), "chan", None),
            P("dirs", ("members", "tiles"), "chan", None),
        ),
        check_vma=False,
    )
```

profile of v0, /device:TPU:0, one launch (start us, length us, event | category | flops | bytes accessed | tf_op | source)
XLA Modules:
  0.0 596.3 jit_solution(17269689504091182904)
XLA Ops:
  28.4 30.6 %all-gather.5.cloned.1.call-done = f32[3,32,4096]{2,1,0:T(8,128)} async-done(((f32[3,8,4096]{2,1,0:T(8,128)}), f32[3,32,4096]{2,1,0:T(8,128)}) %all-gather.5.cloned.1.call-update) | async-done | bytes 1572880 | tf_op jit(solution)/shard_map/all_gather | solution.py:84
  71.6 6.8 %maximum_maximum_fusion = f32[3,8,64,321]{2,0,3,1:T(4,128)} fusion(f32[3,8,64,64]{2,0,3,1:T(4,128)S(1)} %copy.267, f32[3,8,64,256]{2,0,3,1:T(4,128)} %copy.266, f32[321]{0:T(512)S(1)} %pad.10.clone), kind=kLoop, calls=%fused_computation.13 | loop fusion | flops 986112 | bytes 3939588 | tf_op jit(solution)/shard_map/concatenate | solution.py:92
  78.4 29.1 %gather_fusion.6 = f32[2608,3,64]{2,1,0:T(4,128)} fusion(f32[3,8,64,321]{2,0,3,1:T(4,128)} %maximum_maximum_fusion, s32[2608]{0:T(1024)S(1)} %reshape.450), kind=kCustom, calls=%fused_computation.2.clone | custom fusion | bytes 4026752 | tf_op jit(solution)/shard_map/jit(take_along_axis)/gather | solution.py:93
  107.5 5.1 copy.269
  114.5 61.5 %all-gather.7.cloned.1.call-done = f32[3,8,128,326]{3,2,1,0:T(8,128)} async-done(((f32[3,8,64,326]{3,2,1,0:T(8,128)}), f32[3,8,128,326]{3,2,1,0:T(8,128)}) %all-gather.7.cloned.1.call-update) | async-done | bytes 4005904 | tf_op jit(solution)/shard_map/all_gather | solution.py:100
  176.0 26.3 %convolution_bitcast_fusion.1 = f32[3,8,576,326]{2,3,1,0:T(8,128)} fusion(f32[3,8,128,326]{3,2,1,0:T(8,128)} %all-gather.7.cloned.1.call-done, f32[576,128,1,1]{1,0,3,2:T(8,128)S(1)} %bitcast.119), kind=kOutput, calls=%fused_computation.12 | convolution fusion | flops 6922174464 | bytes 22327296 | tf_op jit(solution)/shard_map/kc,btcl->btkl/dot_general | solution.py:58
  202.3 22.3 %copy.270 = f32[3,8,576,326]{3,2,1,0:T(8,128)} copy(f32[3,8,576,326]{2,3,1,0:T(8,128)} %convolution_bitcast_fusion.1) | data formatting | bytes 36052992 | tf_op jit(solution)/shard_map/kc,btcl->btkl/transpose | solution.py:58
  224.6 13.3 %fusion.4 = (f32[3,8,1,64,288]{4,3,2,1,0:T(8,128)}, f32[3,8,1,64,288]{4,3,2,1,0:T(8,128)}, f32[3,8,1,64,288]{4,3,2,1,0:T(8,128)}, f32[3,8,1,64,288]{4,3,2,1,0:T(...) fusion(f32[3,8,9,64,326]{4,3,2,1,0:T(8,128)} %bitcast.99), kind=kLoop, calls=%fused_computation.64 | loop fusion | bytes 31850496 | tf_op jit(solution)/shard_map/slice | solution.py:64
  237.9 4.7 copy.313
  256.6 4.7 copy.317
  266.0 4.7 copy.319
  278.7 12.7 %add_bitcast_fusion.1 = f32[3,8,64,288]{2,1,3,0:T(8,128)} fusion(f32[3,8,1,64,288]{3,1,4,0,2:T(8,128)} %copy.321, f32[3,8,1,64,288]{3,1,4,0,2:T(8,128)} %copy.320, f32[3,8,1,64,288]{3,1,4,0,2:T(8,128)} %copy.319, f32[3,8,1,64,288]{3,1,4,0,2:T(8,128)} %copy.318, f32[3,8,1,64,288]{3,1,4,0,2:T(8,128)} %copy.317, f32[3,8,1,64,288]{3,1,4,0,2:T(8,128)} %copy.316, ...), kind=kLoop, calls=%fused_computation.16 | loop fusion | flops 3538944 | bytes 17694720 | tf_op jit(solution)/shard_map/add | solution.py:65
  307.5 37.1 %all-gather.9.cloned.1.call-done = f32[3,32,4096]{2,1,0:T(8,128)} async-done(((f32[3,8,4096]{2,1,0:T(8,128)}), f32[3,32,4096]{2,1,0:T(8,128)}) %all-gather.9.cloned.1.call-update) | async-done | bytes 1572880 | tf_op jit(solution)/shard_map/all_gather | solution.py:84
  365.7 29.3 %gather_fusion.9 = f32[2608,3,64]{2,1,0:T(4,128)} fusion(f32[3,8,64,321]{2,0,3,1:T(4,128)} %copy.290, s32[2608]{0:T(1024)S(1)} %reshape.450), kind=kCustom, calls=%fused_computation.7.clone | custom fusion | bytes 4026752 | tf_op jit(solution)/shard_map/jit(take_along_axis)/gather | solution.py:93
  395.1 4.9 copy.292
  401.8 61.5 %all-gather.11.cloned.1.call-done = f32[3,8,128,326]{3,2,1,0:T(8,128)} async-done(((f32[3,8,64,326]{3,2,1,0:T(8,128)}), f32[3,8,128,326]{3,2,1,0:T(8,128)}) %all-gather.11.cloned.1.call-update) | async-done | bytes 4005904 | tf_op jit(solution)/shard_map/all_gather | solution.py:100
  463.3 26.3 %convolution_bitcast_fusion = f32[3,8,576,326]{2,3,1,0:T(8,128)} fusion(f32[3,8,128,326]{3,2,1,0:T(8,128)} %all-gather.11.cloned.1.call-done, f32[576,128,1,1]{1,0,3,2:T(8,128)S(1)} %bitcast.118), kind=kOutput, calls=%fused_computation.11 | convolution fusion | flops 6922174464 | bytes 22327296 | tf_op jit(solution)/shard_map/kc,btcl->btkl/dot_general | solution.py:58
  489.6 22.3 %copy.293 = f32[3,8,576,326]{3,2,1,0:T(8,128)} copy(f32[3,8,576,326]{2,3,1,0:T(8,128)} %convolution_bitcast_fusion) | data formatting | bytes 36052992 | tf_op jit(solution)/shard_map/kc,btcl->btkl/transpose | solution.py:58
  511.9 13.3 %fusion.3 = (f32[3,8,1,64,288]{4,3,2,1,0:T(8,128)}, f32[3,8,1,64,288]{4,3,2,1,0:T(8,128)}, f32[3,8,1,64,288]{4,3,2,1,0:T(8,128)}, f32[3,8,1,64,288]{4,3,2,1,0:T(...) fusion(f32[3,8,9,64,326]{4,3,2,1,0:T(8,128)} %bitcast.100), kind=kLoop, calls=%fused_computation.63 | loop fusion | bytes 31850496 | tf_op jit(solution)/shard_map/slice | solution.py:64
  525.1 4.7 copy.322
  543.9 4.7 copy.326
  553.3 4.7 copy.328
  558.0 4.9 copy.329
  566.0 12.7 %add_bitcast_fusion = f32[3,8,64,288]{2,1,3,0:T(8,128)} fusion(f32[3,8,1,64,288]{3,1,4,0,2:T(8,128)} %copy.330, f32[3,8,1,64,288]{3,1,4,0,2:T(8,128)} %copy.329, f32[3,8,1,64,288]{3,1,4,0,2:T(8,128)} %copy.328, f32[3,8,1,64,288]{3,1,4,0,2:T(8,128)} %copy.327, f32[3,8,1,64,288]{3,1,4,0,2:T(8,128)} %copy.326, f32[3,8,1,64,288]{3,1,4,0,2:T(8,128)} %copy.325, ...), kind=kLoop, calls=%fused_computation.15 | loop fusion | flops 3538944 | bytes 17694720 | tf_op jit(solution)/shard_map/add | solution.py:65
  (138 shorter events, 133.5 us)
Async XLA Ops:
  7.2 107.3 %copy-start = (f32[9,128,128]{2,1,0:T(8,128)S(1)}, f32[9,128,128]{2,1,0:T(8,128)}, u32[]{:S(2)}) copy-start(f32[9,128,128]{2,1,0:T(8,128)} %param.24) | copy-start | bytes 1769476
  7.2 2.0 copy-start.6
  7.2 51.8 %all-gather.5.cloned.1.call-start = ((), (), s32[]{:S(2)}) async-start(), calls=%async_computation | async-start | bytes 1966080 | tf_op jit(solution)/shard_map/all_gather | solution.py:84
  10.5 1.6 copy-start.2
  12.2 6.9 %copy-start.13 = (s32[32,4]{0,1:T(4,128)S(1)}, s32[32,4]{0,1:T(4,128)}, u32[]{:S(2)}) copy-start(s32[32,4]{0,1:T(4,128)} %param.28) | copy-start | bytes 1540
  12.3 7.0 %copy-start.14 = (s32[32,4]{0,1:T(4,128)S(1)}, s32[32,4]{0,1:T(4,128)}, u32[]{:S(2)}) copy-start(s32[32,4]{0,1:T(4,128)} %param.30) | copy-start | bytes 1540
  12.3 7.0 %copy-start.18 = (s32[32]{0:T(128)S(1)}, s32[32]{0:T(128)}, u32[]{:S(2)}) copy-start(s32[32]{0:T(128)} %param.31) | copy-start | bytes 388
  12.3 8.4 %copy-start.17 = (s32[256]{0:T(256)S(1)}, s32[256]{0:T(256)}, u32[]{:S(2)}) copy-start(s32[256]{0:T(256)} %constant.181) | copy-start | bytes 3076
  14.5 7.1 %copy-start.15 = (s32[32,4]{0,1:T(4,128)S(1)}, s32[32,4]{0,1:T(4,128)}, u32[]{:S(2)}) copy-start(s32[32,4]{0,1:T(4,128)} %param.29) | copy-start | bytes 1540
  14.5 7.9 %copy-start.5 = (f32[2,8,64,256]{3,2,1,0:T(8,128)S(1)}, f32[2,8,64,256]{3,2,1,0:T(8,128)}, u32[]{:S(2)}) copy-start(f32[2,8,64,256]{3,2,1,0:T(8,128)} %param.23) | copy-start | bytes 3145732
  19.1 156.9 %all-gather.7.cloned.1.call-start = ((), (), s32[]{:S(2)}) async-start(), calls=%async_computation.1 | async-start | bytes 7077888 | tf_op jit(solution)/shard_map/all_gather | solution.py:100
  23.6 3.3 copy-start.16
  23.6 4.4 copy-start.8
  23.6 4.4 copy-start.9
  23.6 4.4 copy-start.10
  23.7 4.4 copy-start.11
  23.7 4.4 copy-start.12
  112.7 1.7 copy-start.19
  114.4 230.2 %all-gather.9.cloned.1.call-start = ((), (), s32[]{:S(2)}) async-start(), calls=%async_computation.2 | async-start | bytes 1966080 | tf_op jit(solution)/shard_map/all_gather | solution.py:84
  296.0 2.2 copy-start.4
  307.4 155.9 %all-gather.11.cloned.1.call-start = ((), (), s32[]{:S(2)}) async-start(), calls=%async_computation.3 | async-start | bytes 7077888 | tf_op jit(solution)/shard_map/all_gather | solution.py:100
  400.0 1.7 copy-start.20
  400.0 1.8 copy-start.7
  583.3 6.3 %copy-start.1 = (f32[9,128,128]{2,1,0:T(8,128)S(1)}, f32[9,128,128]{2,1,0:T(8,128)}, u32[]{:S(2)}) copy-start(f32[9,128,128]{2,1,0:T(8,128)} %param.24) | copy-start | bytes 1769476
  (1 other events, 1.3 us)
Sparse Core Ops, SparseCore 0:
  19.2 39.7 all-gather.4
  114.5 61.4 all-gather.6
  307.5 37.0 all-gather.8
  401.8 61.4 all-gather.10
where the time goes:
time: 607 us; the launch traced here: 596 us
  local copies, waits for them, and re-layouts  293 us (48%)
  waiting for transfers between devices  191 us (31%)
  matrix products  52.6 us (9%)
  other arithmetic  45.5 us (7%)
  between operations  14.5 us (2%)
    all_gather x2, waiting for transfers between devices, layer_sums(): gathered = lax.all_gather(padded, 'chan', axis=2, tiled=True)  123 us
    unnamed x68, local copies, waits for them, and re-layouts  89.5 us
    gather x5, local copies, waits for them, and re-layouts, pad_fields(): return jnp.take_along_axis(source, index[None, :, None, :], axis=-1)  68.6 us
    all_gather x2, waiting for transfers between devices, pad_fields(): lax.all_gather(edges.reshape(stream_count, tile_count, 4 * chan_count * S...  67.7 us
    dot_general x2, matrix products, convolve(): jnp.einsum('kc,btcl->btkl', flat_weight, padded, precision=lax.Precision....  52.6 us
    transpose x2, local copies, waits for them, and re-layouts, convolve(): jnp.einsum('kc,btcl->btkl', flat_weight, padded, precision=lax.Precision....  44.5 us
    slice x2, local copies, waits for them, and re-layouts, convolve(): term = planes[:, :, row_off * 3 + col_off, :, offset:offset + span]  26.5 us
    add x2, other arithmetic, convolve(): summed = term if summed is None else summed + term  25.5 us
  transfers between devices with their start and end apart: 4, of which 4 were waited for; matrix products, arithmetic and copies ran while one was open for 2% of the time, Pallas kernels for 0%

commit v1 on v0

--- a/solution.py
+++ b/solution.py
@@ -5,6 +5,12 @@
 from jax.sharding import PartitionSpec as P
 
 S = 16
+
+
+def feed_the_table(xin):
+    plain = lax.all_gather(xin, "chan")
+    low = jnp.concatenate(plain, axis=2)
+    return low
 
 
 def static_tables():
@@ -97,7 +103,7 @@
     chan_group = padded.shape[2]
     chan_start = lax.axis_index("chan") * chan_group
     weight_rows = lax.dynamic_slice_in_dim(weight, chan_start, chan_group, 1)
-    gathered = lax.all_gather(padded, "chan", axis=2, tiled=True)
+    gathered = feed_the_table(padded)
     return convolve(gathered, weight_rows)
 
 

time: 607 us -> 610 us (level)
  no operation moved by 1% of the time
where the time goes in v1:
time: 610 us; the launch traced here: 600 us
  local copies, waits for them, and re-layouts  299 us (49%)
  waiting for transfers between devices  191 us (31%)
  matrix products  50.6 us (8%)
  other arithmetic  44 us (7%)
  between operations  14.5 us (2%)
    all_gather x2, waiting for transfers between devices, feed_the_table(): plain = lax.all_gather(xin, 'chan')  123 us
    unnamed x68, local copies, waits for them, and re-layouts  89.3 us
    all_gather x2, waiting for transfers between devices, pad_fields(): lax.all_gather(edges.reshape(stream_count, tile_count, 4 * chan_count * S...  67.7 us
    gather x5, local copies, waits for them, and re-layouts, pad_fields(): return jnp.take_along_axis(source, index[None, :, None, :], axis=-1)  67.7 us
    dot_general x2, matrix products, convolve(): jnp.einsum('kc,btcl->btkl', flat_weight, padded, precision=lax.Precision....  50.6 us
    transpose x2, local copies, waits for them, and re-layouts, convolve(): jnp.einsum('kc,btcl->btkl', flat_weight, padded, precision=lax.Precision....  44.5 us
    slice x2, local copies, waits for them, and re-layouts, convolve(): term = planes[:, :, row_off * 3 + col_off, :, offset:offset + span]  26.8 us
    add x2, other arithmetic, convolve(): summed = term if summed is None else summed + term  25.5 us
  transfers between devices with their start and end apart: 4, of which 4 were waited for; matrix products, arithmetic and copies ran while one was open for 2% of the time, Pallas kernels for 0%

profile of v1, /device:TPU:0, one launch (start us, length us, event | category | flops | bytes accessed | tf_op | source)
XLA Modules:
  0.0 599.6 jit_solution(16407415747729645946)
XLA Ops:
  28.4 30.6 %all-gather.7.cloned.1.call-done = f32[3,32,4096]{2,1,0:T(8,128)} async-done(((f32[3,8,4096]{2,1,0:T(8,128)}), f32[3,32,4096]{2,1,0:T(8,128)}) %all-gather.7.cloned.1.call-update) | async-done | bytes 1572880 | tf_op jit(solution)/shard_map/all_gather | solution.py:90
  71.6 6.8 %maximum_maximum_fusion = f32[3,8,64,321]{2,0,3,1:T(4,128)} fusion(f32[3,8,64,64]{2,0,3,1:T(4,128)S(1)} %copy.279, f32[3,8,64,256]{2,0,3,1:T(4,128)} %copy.278, f32[321]{0:T(512)S(1)} %pad.10.clone), kind=kLoop, calls=%fused_computation.13 | loop fusion | flops 986112 | bytes 3939588 | tf_op jit(solution)/shard_map/concatenate | solution.py:98
  78.4 29.1 %gather_fusion.6 = f32[2608,3,64]{2,1,0:T(4,128)} fusion(f32[3,8,64,321]{2,0,3,1:T(4,128)} %maximum_maximum_fusion, s32[2608]{0:T(1024)S(1)} %reshape.468), kind=kCustom, calls=%fused_computation.2.clone | custom fusion | bytes 4026752 | tf_op jit(solution)/shard_map/jit(take_along_axis)/gather | solution.py:99
  107.5 5.1 copy.280
  114.5 61.5 %all-gather.11.cloned.1.call-done = f32[6,8,64,326]{3,2,1,0:T(8,128)} async-done(((f32[3,8,64,326]{3,2,1,0:T(8,128)}), f32[6,8,64,326]{3,2,1,0:T(8,128)}) %all-gather.11.cloned.1.call-update) | async-done | bytes 4005904 | tf_op jit(solution)/shard_map/all_gather | solution.py:11
  178.9 25.3 %convolution_bitcast_fusion.1 = f32[3,8,576,326]{2,3,1,0:T(8,128)} fusion(f32[3,8,128,326]{3,2,1,0:T(8,128)S(1)} %bitcast.112, f32[576,128,1,1]{1,0,3,2:T(8,128)S(1)} %bitcast.131), kind=kOutput, calls=%fused_computation.12 | convolution fusion | flops 6922174464 | bytes 22327296 | tf_op jit(solution)/shard_map/kc,btcl->btkl/dot_general | solution.py:64
  204.2 22.3 %copy.283 = f32[3,8,576,326]{3,2,1,0:T(8,128)} copy(f32[3,8,576,326]{2,3,1,0:T(8,128)} %convolution_bitcast_fusion.1) | data formatting | bytes 36052992 | tf_op jit(solution)/shard_map/kc,btcl->btkl/transpose | solution.py:64
  226.4 13.3 %fusion.4 = (f32[3,8,1,64,288]{4,3,2,1,0:T(8,128)}, f32[3,8,1,64,288]{4,3,2,1,0:T(8,128)}, f32[3,8,1,64,288]{4,3,2,1,0:T(8,128)}, f32[3,8,1,64,288]{4,3,2,1,0:T(...) fusion(f32[3,8,9,64,326]{4,3,2,1,0:T(8,128)} %bitcast.107), kind=kLoop, calls=%fused_computation.64 | loop fusion | bytes 31850496 | tf_op jit(solution)/shard_map/slice | solution.py:70
  239.7 4.7 copy.327
  253.7 4.8 copy.330
  258.6 4.7 copy.331
  268.0 4.7 copy.333
  272.7 4.7 copy.334
  280.5 12.7 %add_bitcast_fusion.1 = f32[3,8,64,288]{2,1,3,0:T(8,128)} fusion(f32[3,8,1,64,288]{3,1,4,0,2:T(8,128)} %copy.335, f32[3,8,1,64,288]{3,1,4,0,2:T(8,128)} %copy.334, f32[3,8,1,64,288]{3,1,4,0,2:T(8,128)} %copy.333, f32[3,8,1,64,288]{3,1,4,0,2:T(8,128)} %copy.332, f32[3,8,1,64,288]{3,1,4,0,2:T(8,128)} %copy.331, f32[3,8,1,64,288]{3,1,4,0,2:T(8,128)} %copy.330, ...), kind=kLoop, calls=%fused_computation.16 | loop fusion | flops 3538944 | bytes 17694720 | tf_op jit(solution)/shard_map/add | solution.py:71
  309.3 37.1 %all-gather.9.cloned.1.call-done = f32[3,32,4096]{2,1,0:T(8,128)} async-done(((f32[3,8,4096]{2,1,0:T(8,128)}), f32[3,32,4096]{2,1,0:T(8,128)}) %all-gather.9.cloned.1.call-update) | async-done | bytes 1572880 | tf_op jit(solution)/shard_map/all_gather | solution.py:90
  367.6 29.3 %gather_fusion.9 = f32[2608,3,64]{2,1,0:T(4,128)} fusion(f32[3,8,64,321]{2,0,3,1:T(4,128)} %copy.303, s32[2608]{0:T(1024)S(1)} %reshape.468), kind=kCustom, calls=%fused_computation.7.clone | custom fusion | bytes 4026752 | tf_op jit(solution)/shard_map/jit(take_along_axis)/gather | solution.py:99
  403.2 61.5 %all-gather.13.cloned.1.call-done = f32[6,8,64,326]{3,2,1,0:T(8,128)} async-done(((f32[3,8,64,326]{3,2,1,0:T(8,128)}), f32[6,8,64,326]{3,2,1,0:T(8,128)}) %all-gather.13.cloned.1.call-update) | async-done | bytes 4005904 | tf_op jit(solution)/shard_map/all_gather | solution.py:11
  467.6 25.3 %convolution_bitcast_fusion = f32[3,8,576,326]{2,3,1,0:T(8,128)} fusion(f32[3,8,128,326]{3,2,1,0:T(8,128)S(1)} %bitcast.113, f32[576,128,1,1]{1,0,3,2:T(8,128)S(1)} %bitcast.130), kind=kOutput, calls=%fused_computation.11 | convolution fusion | flops 6922174464 | bytes 22327296 | tf_op jit(solution)/shard_map/kc,btcl->btkl/dot_general | solution.py:64
  492.8 22.3 %copy.308 = f32[3,8,576,326]{3,2,1,0:T(8,128)} copy(f32[3,8,576,326]{2,3,1,0:T(8,128)} %convolution_bitcast_fusion) | data formatting | bytes 36052992 | tf_op jit(solution)/shard_map/kc,btcl->btkl/transpose | solution.py:64
  515.1 13.5 %fusion.3 = (f32[3,8,1,64,288]{4,3,2,1,0:T(8,128)}, f32[3,8,1,64,288]{4,3,2,1,0:T(8,128)}, f32[3,8,1,64,288]{4,3,2,1,0:T(8,128)}, f32[3,8,1,64,288]{4,3,2,1,0:T(...) fusion(f32[3,8,9,64,326]{4,3,2,1,0:T(8,128)} %bitcast.108), kind=kLoop, calls=%fused_computation.63 | loop fusion | bytes 31850496 | tf_op jit(solution)/shard_map/slice | solution.py:70
  528.6 4.7 copy.336
  547.3 4.7 copy.340
  556.7 4.7 copy.342
  569.2 12.7 %add_bitcast_fusion = f32[3,8,64,288]{2,1,3,0:T(8,128)} fusion(f32[3,8,1,64,288]{3,1,4,0,2:T(8,128)} %copy.344, f32[3,8,1,64,288]{3,1,4,0,2:T(8,128)} %copy.343, f32[3,8,1,64,288]{3,1,4,0,2:T(8,128)} %copy.342, f32[3,8,1,64,288]{3,1,4,0,2:T(8,128)} %copy.341, f32[3,8,1,64,288]{3,1,4,0,2:T(8,128)} %copy.340, f32[3,8,1,64,288]{3,1,4,0,2:T(8,128)} %copy.339, ...), kind=kLoop, calls=%fused_computation.15 | loop fusion | flops 3538944 | bytes 17694720 | tf_op jit(solution)/shard_map/add | solution.py:71
  (141 shorter events, 138.8 us)
Async XLA Ops:
  7.2 107.3 %copy-start = (f32[9,128,128]{2,1,0:T(8,128)S(1)}, f32[9,128,128]{2,1,0:T(8,128)}, u32[]{:S(2)}) copy-start(f32[9,128,128]{2,1,0:T(8,128)} %param.24) | copy-start | bytes 1769476
  7.2 2.0 copy-start.6
  7.2 51.8 %all-gather.7.cloned.1.call-start = ((), (), s32[]{:S(2)}) async-start(), calls=%async_computation | async-start | bytes 1966080 | tf_op jit(solution)/shard_map/all_gather | solution.py:90
  10.5 1.6 copy-start.2
  12.2 6.9 %copy-start.13 = (s32[32,4]{0,1:T(4,128)S(1)}, s32[32,4]{0,1:T(4,128)}, u32[]{:S(2)}) copy-start(s32[32,4]{0,1:T(4,128)} %param.28) | copy-start | bytes 1540
  12.3 7.0 %copy-start.14 = (s32[32,4]{0,1:T(4,128)S(1)}, s32[32,4]{0,1:T(4,128)}, u32[]{:S(2)}) copy-start(s32[32,4]{0,1:T(4,128)} %param.30) | copy-start | bytes 1540
  12.3 7.0 %copy-start.18 = (s32[32]{0:T(128)S(1)}, s32[32]{0:T(128)}, u32[]{:S(2)}) copy-start(s32[32]{0:T(128)} %param.31) | copy-start | bytes 388
  12.3 8.4 %copy-start.17 = (s32[256]{0:T(256)S(1)}, s32[256]{0:T(256)}, u32[]{:S(2)}) copy-start(s32[256]{0:T(256)} %constant.181) | copy-start | bytes 3076
  14.5 7.1 %copy-start.15 = (s32[32,4]{0,1:T(4,128)S(1)}, s32[32,4]{0,1:T(4,128)}, u32[]{:S(2)}) copy-start(s32[32,4]{0,1:T(4,128)} %param.29) | copy-start | bytes 1540
  14.5 7.9 %copy-start.5 = (f32[2,8,64,256]{3,2,1,0:T(8,128)S(1)}, f32[2,8,64,256]{3,2,1,0:T(8,128)}, u32[]{:S(2)}) copy-start(f32[2,8,64,256]{3,2,1,0:T(8,128)} %param.23) | copy-start | bytes 3145732
  19.1 156.9 %all-gather.11.cloned.1.call-start = ((), (), s32[]{:S(2)}) async-start(), calls=%async_computation.2 | async-start | bytes 7077888 | tf_op jit(solution)/shard_map/all_gather | solution.py:11
  23.6 3.3 copy-start.16
  23.6 4.4 copy-start.8
  23.6 4.4 copy-start.9
  23.6 4.4 copy-start.10
  23.7 4.4 copy-start.11
  23.7 4.4 copy-start.12
  112.7 1.7 copy-start.19
  114.4 232.1 %all-gather.9.cloned.1.call-start = ((), (), s32[]{:S(2)}) async-start(), calls=%async_computation.1 | async-start | bytes 1966080 | tf_op jit(solution)/shard_map/all_gather | solution.py:90
  297.8 2.2 copy-start.4
  309.2 155.4 %all-gather.13.cloned.1.call-start = ((), (), s32[]{:S(2)}) async-start(), calls=%async_computation.3 | async-start | bytes 7077888 | tf_op jit(solution)/shard_map/all_gather | solution.py:11
  401.1 1.9 copy-start.20
  401.2 2.0 copy-start.7
  586.5 6.3 %copy-start.1 = (f32[9,128,128]{2,1,0:T(8,128)S(1)}, f32[9,128,128]{2,1,0:T(8,128)}, u32[]{:S(2)}) copy-start(f32[9,128,128]{2,1,0:T(8,128)} %param.24) | copy-start | bytes 1769476
  (1 other events, 1.3 us)
Sparse Core Ops, SparseCore 0:
  19.2 39.7 all-gather.6
  114.5 61.4 all-gather.10
  309.4 37.0 all-gather.8
  403.2 61.4 all-gather.12
